TPU v7x, 32 devices: a whole 2x2x4 slice. The times are simulated.
32 devices in a mesh: pipe: 2 (over x), ctx: 4 (over y, core), tp: 4 (over z).
Axes of the slice: x: 2, y: 2, z: 4, core: 2. Of those that a mesh axis runs over, the one named last changes fastest.
Arguments:
- queries: bfloat16 [2, 512, 16384], P('pipe', 'ctx', 'tp'), may hold values from -5 to 5
- key_vectors: bfloat16 [2, 512, 1024], P('pipe', 'ctx', 'tp'), may hold values from -5 to 5
- saved_value_rows: bfloat16 [2, 512, 1024], P('pipe', 'ctx', 'tp'), may hold values from -5 to 5
- output_cotangent: bfloat16 [2, 512, 16384], P('pipe', 'ctx', 'tp'), may hold values from -5 to 5
- layer_input: bfloat16 [2, 512, 8192], P('pipe', 'ctx'), may hold values from -5 to 5
- documents: int32 [2, 512], P('pipe'), may hold values from 0 to 3, as said below
Outputs:
- query_gradient: bfloat16 [2, 512, 16384], P('pipe', 'ctx', 'tp')
- key_gradient: bfloat16 [2, 512, 1024], P('pipe', 'ctx', 'tp')
- value_gradient: bfloat16 [2, 512, 1024], P('pipe', 'ctx', 'tp')
- weight_gradient: float32 [2, 8192, 1024], P('pipe', 'ctx', 'tp')
Inputs may be any that keep to these rules, and one draw needn't show every extreme that they name: For each section, the numbers start at 0 on the first token and never fall along the tokens; each of the 4 documents has one token or more.
All inputs are finite; a program needn't handle non-finite values.
Results may differ from a plain program's by a relative error of at most 0.0095.
Values may be sent and summed in bfloat16 or wider, within the bound.
No kernel may reach another device: no remote copies, remote signals or barrier semaphores. Data moves between devices by JAX's collectives and lax.ppermute only.
A program may use at most 64 MiB of HBM per device.

v0:
```python
import math

import jax
import jax.numpy as jnp
from jax import lax
from jax.sharding import PartitionSpec as P

QUERY_HEADS = 128
KEY_VALUE_HEADS = 8
HEAD_SIZE = 128


def shifted(block, axis, distance):
    devices = range(lax.axis_size(axis))
    route = [((i - distance) % len(devices), i) for i in devices]
    return lax.ppermute(block, axis, route)


def attend(
    query_rows,
    cotangent_rows,
    keys_one,
    values_one,
    query_position,
    query_documents,
    key_documents,
    scaling,
):
    row_count = query_rows.shape[0]
    head_width = query_rows.shape[1]
    block_rows = math.gcd(row_count, 512)
    block_count = row_count // block_rows
    key_count = keys_one.shape[0]
    key_position = jnp.arange(key_count, dtype=jnp.int32)

    def advance(totals, pieces):
        key_total, value_total = totals
        block_query, block_cotangent, block_position, block_documents = pieces
        scores = (
            jnp.einsum("rd,kd->rk", block_query, keys_one, preferred_element_type=jnp.float32)
            * scaling
        )
        allowed = (block_documents[:, None] == key_documents[None, :]) & (
            key_position[None, :] <= block_position[:, None]
        )
        masked = jnp.where(allowed, scores, -1e30)
        row_max = jnp.max(masked, axis=1, keepdims=True)
        raised = jnp.where(allowed, jnp.exp(masked - row_max), 0.0)
        weights = raised / jnp.sum(raised, axis=1, keepdims=True)
        weights_low = weights.astype(jnp.bfloat16)
        attended = jnp.dot(weights_low, values_one, preferred_element_type=jnp.float32)
        row_delta = jnp.sum(block_cotangent.astype(jnp.float32) * attended, axis=1, keepdims=True)
        weights_back = jnp.einsum(
            "rd,kd->rk", block_cotangent, values_one, preferred_element_type=jnp.float32
        )
        scores_back = weights * (weights_back - row_delta)
        scores_low = scores_back.astype(jnp.bfloat16)
        query_part = jnp.dot(scores_low, keys_one, preferred_element_type=jnp.float32) * scaling
        key_total = (
            key_total
            + jnp.einsum("rk,rd->kd", scores_low, block_query, preferred_element_type=jnp.float32)
            * scaling
        )
        value_total = value_total + jnp.einsum(
            "rk,rd->kd", weights_low, block_cotangent, preferred_element_type=jnp.float32
        )
        return ((key_total, value_total), query_part)

    zero_init = jnp.zeros((key_count, head_width), jnp.float32)
    stacked = (
        query_rows.reshape(block_count, block_rows, head_width),
        cotangent_rows.reshape(block_count, block_rows, head_width),
        query_position.reshape(block_count, block_rows),
        query_documents.reshape(block_count, block_rows),
    )
    (key_total, value_total), query_parts = lax.scan(advance, (zero_init, zero_init), stacked)
    return (query_parts.reshape(row_count, head_width), key_total, value_total)


def shards(queries, key_vectors, saved_value_rows, output_cotangent, layer_input, documents):
    incoming = shifted(layer_input[0], "pipe", 1)
    position = lax.axis_index("ctx")
    tokens_here = queries.shape[1]
    local_heads = queries.shape[2] // HEAD_SIZE
    local_kv = key_vectors.shape[2] // HEAD_SIZE
    query_group = QUERY_HEADS // KEY_VALUE_HEADS
    scaling = HEAD_SIZE ** (-0.5)
    query_cube = queries[0].reshape(tokens_here, local_heads, HEAD_SIZE)
    cotangent_cube = output_cotangent[0].reshape(tokens_here, local_heads, HEAD_SIZE)
    key_cube = key_vectors[0].reshape(tokens_here, local_kv, HEAD_SIZE)
    value_cube = saved_value_rows[0].reshape(tokens_here, local_kv, HEAD_SIZE)
    doc_row = documents[0]
    key_all, value_all = (
        lax.all_gather(key_cube, "ctx", axis=0, tiled=True),
        lax.all_gather(value_cube, "ctx", axis=0, tiled=True),
    )
    own_position = position * tokens_here + jnp.arange(tokens_here, dtype=jnp.int32)
    own_documents = lax.dynamic_slice_in_dim(doc_row, position * tokens_here, tokens_here)
    row_position = jnp.tile(own_position, query_group)
    row_documents = jnp.tile(own_documents, query_group)
    query_blocks = []
    key_list = []
    value_list = []
    for kv_index in range(local_kv):
        head_query = query_cube[:, kv_index * query_group : (kv_index + 1) * query_group]
        head_cotangent = cotangent_cube[:, kv_index * query_group : (kv_index + 1) * query_group]
        query_rows = head_query.transpose(1, 0, 2).reshape(query_group * tokens_here, HEAD_SIZE)
        cotangent_rows = head_cotangent.transpose(1, 0, 2).reshape(
            query_group * tokens_here, HEAD_SIZE
        )
        query_flat, key_part, value_part = attend(
            query_rows,
            cotangent_rows,
            key_all[:, kv_index],
            value_all[:, kv_index],
            row_position,
            row_documents,
            doc_row,
            scaling,
        )
        query_blocks.append(
            query_flat.reshape(query_group, tokens_here, HEAD_SIZE).transpose(1, 0, 2)
        )
        key_list.append(key_part)
        value_list.append(value_part)
    query_local = jnp.concatenate(query_blocks, axis=1).astype(jnp.bfloat16)
    key_terms = jnp.stack(key_list, axis=1)
    value_terms = jnp.stack(value_list, axis=1)
    key_sum, value_sum = (
        lax.psum_scatter(key_terms, "ctx", scatter_dimension=0, tiled=True),
        lax.psum_scatter(value_terms, "ctx", scatter_dimension=0, tiled=True),
    )
    key_gradient = key_sum.reshape(tokens_here, local_kv * HEAD_SIZE).astype(jnp.bfloat16)
    value_gradient = value_sum.reshape(tokens_here, local_kv * HEAD_SIZE).astype(jnp.bfloat16)
    query_gradient = query_local.reshape(tokens_here, local_heads * HEAD_SIZE)
    weight_gradient = lax.psum_scatter(
        lax.dot_general(
            incoming, key_gradient, (((0,), (0,)), ((), ())), preferred_element_type=jnp.float32
        ),
        "ctx",
        scatter_dimension=0,
        tiled=True,
    )
    return (query_gradient[None], key_gradient[None], value_gradient[None], weight_gradient[None])


def solution(mesh):
    placed = (
        P("pipe", "ctx", "tp"),
        P("pipe", "ctx", "tp"),
        P("pipe", "ctx", "tp"),
        P("pipe", "ctx", "tp"),
        P("pipe", "ctx", None),
        P("pipe", None),
    )
    return jax.shard_map(
        shards,
        mesh=mesh,
        in_specs=placed,
        out_specs=(
            P("pipe", "ctx", "tp"),
            P("pipe", "ctx", "tp"),
            P("pipe", "ctx", "tp"),
            P("pipe", "ctx", "tp"),
        ),
        check_vma=False,
    )
```

profile of v0, /device:TPU:0, one launch (start us, length us, event | category | flops | bytes accessed | tf_op | source)
XLA Modules:
  0.0 196.5 jit_solution(5464776909380908533)
XLA Ops:
  7.2 3.0 %collective-permute-start = (bf16[128,8192]{1,0:T(8,128)(2,1)}, bf16[128,8192]{1,0:T(8,128)(2,1)}, u32[]{:S(2)}, u32[]{:S(2)}) collective-permute-start(bf16[128,8192]{1,0:T(8,128)(2,1)} %bitcast.202), channel_id=1, source_target_pairs={{16,0},{0,16},{17,1},{1,17},{18,2},{2,18},{19,3},{3,19},{20,4},{4,... | collective-permute-start | bytes 6291464 | tf_op jit(solution)/shard_map/ppermute | solution.py:16
  11.9 1.0 copy.44
  12.8 5.8 %all_gather.7 = bf16[512,2,128]{0,2,1:T(8,128)(2,1)S(1)} all-gather(bf16[128,2,128]{0,2,1:T(8,128)(2,1)S(1)} %bitcast.201), channel_id=1, replica_groups=mesh['pipe'=2,'ctx'=4,'tp'=4] {'ctx'}, dimensions={0}, use_global_device_ids=true | all-gather | bytes 327680 | tf_op jit(solution)/shard_map/all_gather | solution.py:95
  19.0 5.9 %all_gather.6 = bf16[512,2,128]{0,2,1:T(8,128)(2,1)S(1)} all-gather(bf16[128,2,128]{0,2,1:T(8,128)(2,1)S(1)} %bitcast.200), channel_id=1, replica_groups=mesh['pipe'=2,'ctx'=4,'tp'=4] {'ctx'}, dimensions={0}, use_global_device_ids=true | all-gather | bytes 327680 | tf_op jit(solution)/shard_map/all_gather | solution.py:94
  26.7 1.6 copy.42
  28.3 1.0 slice_bitcast_fusion.1
  29.3 1.3 copy.43
  31.5 22.2 %while.30 = (s32[]{:T(128)}, f32[512,128]{1,0:T(8,128)S(1)}, f32[512,128]{1,0:T(8,128)S(1)}, bf16[4,512,128]{2,1,0:T(8,128)(2,1)}, s32[4,512]{1,0:T(4,128)S(1)},...) while((s32[]{:T(128)}, f32[512,128]{1,0:T(8,128)S(1)}, ...), condition=%wide.region_4.5_spmd.clone, body=%wide.region_0.4_spmd.clone.sunk | while | flops 409270784 | bytes 16163036 | solution.py:76
  31.7 1.3 fusion.108
  34.6 1.3 fusion.113
  37.2 1.3 fusion.108
  40.2 1.3 fusion.113
  42.8 1.3 fusion.108
  45.7 1.3 fusion.113
  48.3 1.3 fusion.108
  51.2 1.3 fusion.113
  54.1 11.8 %while.31 = (s32[]{:T(128)}, f32[512,128]{1,0:T(8,128)S(1)}, f32[512,128]{1,0:T(8,128)S(1)}, bf16[4,512,128]{2,1,0:T(8,128)(2,1)S(1)}, s32[4,512]{1,0:T(4,128)S(...) while((s32[]{:T(128)}, f32[512,128]{1,0:T(8,128)S(1)}, ...), condition=%wide.region_9.10_spmd.clone, body=%wide.region_5.9_spmd.clone.sunk | while | flops 409270784 | bytes 11968676 | solution.py:76
  67.9 21.1 %reduce-scatter.4.cloned.1.call-done = f32[128,2,128]{0,2,1:T(8,128)} async-done(((f32[512,2,128]{0,2,1:T(8,128)}), f32[128,2,128]{0,2,1:T(8,128)}) %reduce-scatter.4.cloned.1.call-update) | async-done | bytes 131088 | tf_op jit(solution)/shard_map/reduce_scatter | solution.py:130
  90.0 6.0 %convolution_bitcast_fusion = f32[8192,256]{0,1:T(8,128)} fusion(bf16[128,256]{0,1:T(8,128)(2,1)S(1)} %bitcast.186, bf16[128,8192]{1,0:T(8,128)(2,1)} %collective-permute-done), kind=kOutput, calls=%fused_computation.64 | convolution fusion | flops 536870912 | bytes 10551296 | tf_op jit(solution)/shard_map/dot_general | solution.py:137
  96.1 1.1 copy-done.3
  97.9 1.3 convert_element_type.58
  99.9 13.3 %reduce-scatter.6.cloned.1.call-done = f32[128,2,128]{2,0,1:T(8,128)} async-done(((f32[512,2,128]{2,0,1:T(8,128)}), f32[128,2,128]{2,0,1:T(8,128)}) %reduce-scatter.6.cloned.1.call-update) | async-done | bytes 131088 | tf_op jit(solution)/shard_map/reduce_scatter | solution.py:131
  114.9 72.2 %reduce-scatter.8.cloned.1.call-done = f32[2048,256]{0,1:T(8,128)} async-done(((f32[8192,256]{0,1:T(8,128)}), f32[2048,256]{0,1:T(8,128)}) %reduce-scatter.8.cloned.1.call-update) | async-done | bytes 2097168 | tf_op jit(solution)/shard_map/reduce_scatter | solution.py:136
  187.1 2.9 %copy.59 = f32[1,2048,256]{2,1,0:T(8,128)} copy(f32[1,2048,256]{1,2,0:T(8,128)} %bitcast.174) | data formatting | bytes 4194304
  (145 shorter events, 34.1 us)
Async XLA Ops:
  7.2 18.0 %copy-start.4 = (bf16[1,128,4096]{2,1,0:T(8,128)(2,1)S(1)}, bf16[1,128,4096]{2,1,0:T(8,128)(2,1)}, u32[]{:S(2)}) copy-start(bf16[1,128,4096]{2,1,0:T(8,128)(2,1)} %param.10) | copy-start | bytes 3145732
  7.2 81.9 %reduce-scatter.4.cloned.1.call-start = ((), (), s32[]{:S(2)}) async-start(), calls=%async_computation.3 | async-start | bytes 655360 | tf_op jit(solution)/shard_map/reduce_scatter | solution.py:130
  7.2 82.8 %collective-permute-start = (bf16[128,8192]{1,0:T(8,128)(2,1)}, bf16[128,8192]{1,0:T(8,128)(2,1)}, u32[]{:S(2)}, u32[]{:S(2)}) collective-permute-start(bf16[128,8192]{1,0:T(8,128)(2,1)} %bitcast.202), channel_id=1, source_target_pairs={{16,0},{0,16},{17,1},{1,17},{18,2},{2,18},{19,3},{3,19},{20,4},{4,... | collective-permute-start | bytes 6291464 | tf_op jit(solution)/shard_map/ppermute | solution.py:16
  28.3 3.2 %copy-start.5 = (s32[1,512]{1,0:T(1,128)S(1)}, s32[1,512]{1,0:T(1,128)}, u32[]{:S(2)}) copy-start(s32[1,512]{1,0:T(1,128)} %param.15) | copy-start | bytes 6148
  31.5 22.2 %copy-start = (bf16[16,128,128]{1,2,0:T(8,128)(2,1)S(1)}, bf16[16,128,128]{1,2,0:T(8,128)(2,1)}, u32[]{:S(2)}) copy-start(bf16[16,128,128]{1,2,0:T(8,128)(2,1)} %get-tuple-element.323) | copy-start | bytes 1572868
  34.0 1.9 copy-start.1
  36.3 0.8 copy-start.2
  39.5 1.9 copy-start.1
  41.8 0.8 copy-start.2
  45.0 1.9 copy-start.1
  47.4 0.8 copy-start.2
  50.6 1.9 copy-start.1
  52.9 0.8 copy-start.2
  67.0 46.2 %reduce-scatter.6.cloned.1.call-start = ((), (), s32[]{:S(2)}) async-start(), calls=%async_computation.4 | async-start | bytes 655360 | tf_op jit(solution)/shard_map/reduce_scatter | solution.py:131
  67.9 119.2 %reduce-scatter.8.cloned.1.call-start = ((), (), s32[]{:S(2)}) async-start(), calls=%async_computation.5 | async-start | bytes 10485760 | tf_op jit(solution)/shard_map/reduce_scatter | solution.py:136
  96.0 1.1 copy-start.3
Sparse Core Ops, SparseCore 0:
  67.1 21.9 reduce-scatter.3
  91.5 21.6 reduce-scatter.5
  115.8 71.2 reduce-scatter.7
where the time goes:
time: 197 us
  waiting for transfers between devices  107 us (54%)
  matrix products  29.8 us (15%)
  local copies, waits for them, and re-layouts  21.7 us (11%)
  between operations  13.9 us (7%)
  blocking collectives  11.7 us (6%)
  other arithmetic  8.86 us (4%)
  starting transfers between devices  3.15 us (2%)
    reduce_scatter x1, waiting for transfers between devices, shards(): lax.psum_scatter(lax.dot_general(incoming, key_gradient, (((0,), (0,)), (...  72.2 us
    reduce_scatter x1, waiting for transfers between devices, shards(): lax.psum_scatter(key_terms, 'ctx', scatter_dimension=0, tiled=True)  21.1 us
    reduce_scatter x1, waiting for transfers between devices, shards(): lax.psum_scatter(value_terms, 'ctx', scatter_dimension=0, tiled=True)  13.3 us
    unnamed x20, local copies, waits for them, and re-layouts  10 us
    dot_general x8, matrix products, advance(): jnp.einsum('rd,kd->rk', block_query, keys_one, preferred_element_type=jnp...  6.78 us
    dot_general x8, matrix products, advance(): jnp.einsum('rk,rd->kd', scores_low, block_query, preferred_element_type=j...  6.43 us
    dot_general x1, matrix products, shards(): lax.dot_general(incoming, key_gradient, (((0,), (0,)), ((), ())), preferr...  6.05 us
    all_gather x1, blocking collectives, shards(): lax.all_gather(key_cube, 'ctx', axis=0, tiled=True)  5.91 us
  transfers between devices with their start and end apart: 4, of which 3 were waited for; matrix products, arithmetic and copies ran while one was open for 27% of the time, Pallas kernels for 0%

commit v1 on v0

v1 whole, which is shorter than its diff:
```python
import functools
import math

import jax
import jax.numpy as jnp
from jax import lax
from jax.experimental import pallas as pl
from jax.experimental.pallas import tpu as pltpu
from jax.sharding import PartitionSpec as P

QUERY_HEADS = 128
KEY_VALUE_HEADS = 8
HEAD_SIZE = 128
DOCS = 4

ROWS = (((1,), (1,)), ((), ()))
PLAIN = (((1,), (0,)), ((), ()))
COLUMNS = (((0,), (0,)), ((), ()))


def product(a, b, dims):
    return lax.dot_general(a, b, dims, preferred_element_type=jnp.float32)


def swapped(block, axis, mask):
    count = lax.axis_size(axis)
    return lax.ppermute(block, axis, [(i, i ^ mask) for i in range(count)])


def handed_on(block, section_axis, token_axis, mask):
    sections, count = lax.axis_size(section_axis), lax.axis_size(token_axis)
    route = [
        (s * count + i, ((s + 1) % sections) * count + (i ^ mask))
        for s in range(sections)
        for i in range(count)
    ]
    return lax.ppermute(block, (section_axis, token_axis), route)


def spans(count):
    return [s for s in range(1, count + 1) if s <= 4 or s & (s - 1) == 0 or s == count]


def attention_kernel(
    count,
    group,
    scaling,
    facts,
    query_ref,
    cotangent_ref,
    *rest,
):
    pair_refs = rest[:count]
    query_out, key_keep, key_send, value_keep, value_send = rest[count : count + 5]
    keys, values, keys_turned, bias, key_total, value_total = rest[count + 5 :]
    tokens = query_ref.shape[0]
    step = pl.program_id(1)
    place = facts[0]
    factor = scaling * math.log2(math.e)

    first_block = facts[1]
    needed = place - first_block + 1
    branches = spans(count)

    @pl.when(step == 0)
    def _():
        for slot in range(count):
            row = pl.multiple_of((place ^ slot) * tokens, tokens)
            keys[pl.ds(row, tokens), :] = pair_refs[slot][:tokens, :]
            values[pl.ds(row, tokens), :] = pair_refs[slot][tokens:, :]
        key_total[...] = jnp.zeros_like(key_total)
        value_total[...] = jnp.zeros_like(value_total)

    def work(span):
        start_block = jnp.minimum(first_block, count - span)
        start = pl.multiple_of(start_block * tokens, tokens)
        length = span * tokens
        window = pl.ds(start, length)

        @pl.when(step == 0)
        def _():
            key_position = start + lax.broadcasted_iota(jnp.int32, (length, tokens), 0)
            query_position = place * tokens + lax.broadcasted_iota(jnp.int32, (length, tokens), 1)
            opening = jnp.zeros((length, tokens), jnp.int32)
            for d in range(DOCS - 1):
                bound = facts[2 + d]
                opening = jnp.where(query_position >= bound, jnp.maximum(opening, bound), opening)
            allowed = (key_position <= query_position) & (key_position >= opening)
            bias[:length, :] = jnp.where(allowed, 0.0, -1e30)
            keys_turned[:, :length] = keys[window, :].astype(jnp.float32).T.astype(jnp.bfloat16)

        key_rows = keys[window, :]
        value_rows = values[window, :]
        rows = [slice(g * HEAD_SIZE, (g + 1) * HEAD_SIZE) for g in range(group)]
        query_rows = jnp.concatenate([query_ref[:, r] for r in rows], axis=0)
        cotangent_rows = jnp.concatenate([cotangent_ref[:, r] for r in rows], axis=0)
        scores_all = product(key_rows, query_rows, ROWS)
        back_all = product(value_rows, cotangent_rows, ROWS)
        low_list = []
        back_list = []
        for g in range(group):
            lanes = slice(g * tokens, (g + 1) * tokens)
            scores = scores_all[:, lanes] + bias[:length, :]
            top = jnp.max(scores, axis=0, keepdims=True)
            raised = jnp.exp2((scores - top) * factor)
            weights = raised * (1.0 / jnp.sum(raised, axis=0, keepdims=True))
            back = back_all[:, lanes]
            delta = jnp.sum(weights * back, axis=0, keepdims=True)
            low_list.append(weights.astype(jnp.bfloat16))
            back_list.append((weights * (back - delta)).astype(jnp.bfloat16))
        weights_low = jnp.concatenate(low_list, axis=1)
        scores_low = jnp.concatenate(back_list, axis=1)
        value_total[window, :] += product(weights_low, cotangent_rows, PLAIN)
        key_total[window, :] += product(scores_low, query_rows, PLAIN)
        turned = product(keys_turned[:, :length], scores_low, PLAIN) * scaling
        for g in range(group):
            query_out[:, rows[g]] = turned[:, g * tokens : (g + 1) * tokens].T.astype(
                query_out.dtype
            )

    for i, span in enumerate(branches):
        below = branches[i - 1] if i else 0
        pl.when((needed > below) & (needed <= span))(functools.partial(work, span))

    @pl.when(step == pl.num_programs(1) - 1)
    def _():
        for slot in range(count):
            row = pl.multiple_of((place ^ slot) * tokens, tokens)
            half = pl.ds((slot // 2) * tokens, tokens)
            key_out, value_out = (key_send, value_send) if slot % 2 else (key_keep, value_keep)
            key_out[half, :] = (key_total[pl.ds(row, tokens), :] * scaling).astype(key_out.dtype)
            value_out[half, :] = value_total[pl.ds(row, tokens), :].astype(value_out.dtype)


def attention(facts, queries, cotangent, pairs, scaling, group):
    tokens = queries.shape[0]
    count = len(pairs)
    local_kv = pairs[0].shape[1] // HEAD_SIZE
    per_kv = queries.shape[1] // HEAD_SIZE // local_kv
    groups = per_kv // group
    wide = group * HEAD_SIZE
    half = count // 2 * tokens
    by_head = pl.BlockSpec((tokens, wide), lambda e, g, f: (0, e * groups + g))
    by_kv = pl.BlockSpec((2 * tokens, HEAD_SIZE), lambda e, g, f: (0, e))
    terms = pl.BlockSpec((half, HEAD_SIZE), lambda e, g, f: (0, e))
    term_shape = (half, local_kv * HEAD_SIZE)
    heads = local_kv * per_kv
    work = heads * tokens * tokens * count * HEAD_SIZE
    return pl.pallas_call(
        functools.partial(attention_kernel, count, group, scaling),
        grid_spec=pltpu.PrefetchScalarGridSpec(
            num_scalar_prefetch=1,
            grid=(local_kv, groups),
            in_specs=[by_head, by_head] + [by_kv] * count,
            out_specs=[by_head, terms, terms, terms, terms],
            scratch_shapes=[
                pltpu.VMEM((count * tokens, HEAD_SIZE), jnp.bfloat16),
                pltpu.VMEM((count * tokens, HEAD_SIZE), jnp.bfloat16),
                pltpu.VMEM((HEAD_SIZE, count * tokens), jnp.bfloat16),
                pltpu.VMEM((count * tokens, tokens), jnp.float32),
                pltpu.VMEM((count * tokens, HEAD_SIZE), jnp.float32),
                pltpu.VMEM((count * tokens, HEAD_SIZE), jnp.float32),
            ],
        ),
        out_shape=[
            jax.ShapeDtypeStruct(queries.shape, queries.dtype),
            jax.ShapeDtypeStruct(term_shape, jnp.float32),
            jax.ShapeDtypeStruct(term_shape, jnp.bfloat16),
            jax.ShapeDtypeStruct(term_shape, jnp.float32),
            jax.ShapeDtypeStruct(term_shape, jnp.bfloat16),
        ],
        compiler_params=pltpu.CompilerParams(dimension_semantics=("arbitrary", "arbitrary")),
        cost_estimate=pl.CostEstimate(
            flops=10 * work,
            transcendentals=work // HEAD_SIZE,
            bytes_accessed=6 * queries.size + 16 * half * local_kv * HEAD_SIZE,
        ),
        name="attention_back",
    )(facts, queries, cotangent, *pairs)


def weight_kernel(count, *refs):
    incoming_refs, key_refs, out = refs[:count], refs[count:-1], refs[-1]
    per_ref = count // len(key_refs)
    tokens = incoming_refs[0].shape[0]
    total = None
    for slot in range(count):
        block = slot % per_ref
        key_rows = key_refs[slot // per_ref][block * tokens : (block + 1) * tokens, :]
        term = product(incoming_refs[slot][...], key_rows, COLUMNS)
        total = term if total is None else total + term
    out[...] = total


def weight_product(incoming, key_parts, tile):
    tokens, features = incoming[0].shape
    width = key_parts[0].shape[1]
    return pl.pallas_call(
        functools.partial(weight_kernel, len(incoming)),
        grid=(features // tile,),
        in_specs=[pl.BlockSpec((tokens, tile), lambda i: (0, i)) for _ in incoming]
        + [pl.BlockSpec(k.shape, lambda i: (0, 0)) for k in key_parts],
        out_specs=pl.BlockSpec((tile, width), lambda i: (i, 0)),
        out_shape=jax.ShapeDtypeStruct((features, width), jnp.float32),
        compiler_params=pltpu.CompilerParams(dimension_semantics=("arbitrary",)),
        cost_estimate=pl.CostEstimate(
            flops=2 * len(incoming) * tokens * features * width,
            transcendentals=0,
            bytes_accessed=2 * len(incoming) * tokens * features + 4 * features * width,
        ),
        name="weight_product",
    )(*incoming, *key_parts)


def shards(queries, key_vectors, saved_value_rows, output_cotangent, layer_input, documents):
    count = lax.axis_size("ctx")
    place = lax.axis_index("ctx")
    tokens = queries.shape[1]
    scaling = HEAD_SIZE ** (-0.5)
    features = layer_input.shape[2] // count

    pairs = {0: jnp.concatenate([key_vectors[0], saved_value_rows[0]], axis=0)}
    bits = [1 << b for b in range(count.bit_length() - 1)]
    for bit in reversed(bits):
        for slot in sorted(pairs):
            pairs[slot | bit] = swapped(pairs[slot], "ctx", bit)

    incoming = {}
    for slot in reversed(range(count)):
        block = lax.dynamic_slice_in_dim(layer_input[0], (place ^ slot) * features, features, axis=1)
        incoming[slot] = handed_on(block, "pipe", "ctx", slot)

    numbers = documents[0]
    bounds = jnp.sum(numbers[None, :] < jnp.arange(1, DOCS)[:, None], axis=1, dtype=jnp.int32)
    first = jnp.max(jnp.where(bounds <= place * tokens, bounds, 0)) // tokens
    facts = jnp.concatenate([jnp.stack([place, first]).astype(jnp.int32), bounds])

    query_gradient, key_keep, key_send, value_keep, value_send = attention(
        facts, queries[0], output_cotangent[0], [pairs[s] for s in range(count)], scaling, 4
    )

    stride = key_keep.shape[1]
    for bit in bits:
        blocks = key_keep.shape[0] // tokens
        if bit > 1:
            split_key = key_keep.reshape(blocks // 2, 2, tokens, stride)
            split_value = value_keep.reshape(blocks // 2, 2, tokens, stride)
            key_keep, key_send = (split_key[:, b].reshape(-1, stride) for b in (0, 1))
            value_keep, value_send = (split_value[:, b].reshape(-1, stride) for b in (0, 1))
        if bit == bits[-1]:
            break
        got_key = swapped(key_send.astype(jnp.bfloat16), "ctx", bit)
        got_value = swapped(value_send.astype(jnp.bfloat16), "ctx", bit)
        key_keep = key_keep + got_key.astype(jnp.float32)
        value_keep = value_keep + got_value.astype(jnp.float32)
    top = bits[-1]
    both = jnp.concatenate([key_send, key_keep], axis=0).astype(jnp.bfloat16)
    key_both = jnp.concatenate([key_keep, key_send], axis=0) + swapped(both, "ctx", top)
    key_both = key_both.astype(jnp.bfloat16)
    value_sum = value_keep + swapped(value_send.astype(jnp.bfloat16), "ctx", top)
    key_gradient = key_both[:tokens]
    value_gradient = value_sum.astype(jnp.bfloat16)

    key_parts = {0: key_both}
    for bit in reversed(bits[:-1]):
        for slot in sorted(key_parts):
            key_parts[slot | bit] = swapped(key_parts[slot], "ctx", bit)
    order = [base | extra for base in sorted(key_parts) for extra in (0, top)]
    weight_gradient = weight_product(
        [incoming[s] for s in order],
        [key_parts[b] for b in sorted(key_parts)],
        math.gcd(features, 256),
    )
    return (query_gradient[None], key_gradient[None], value_gradient[None], weight_gradient[None])


def solution(mesh):
    split = P("pipe", "ctx", "tp")
    return jax.shard_map(
        shards,
        mesh=mesh,
        in_specs=(split, split, split, split, P("pipe", "ctx", None), P("pipe", None)),
        out_specs=(split, split, split, split),
        check_vma=False,
    )
```

time: 197 us -> 82.4 us (0.42)
  waiting for transfers between devices: 107 us -> 41.7 us
  matrix products: 29.8 us -> 0 us
  local copies, waits for them, and re-layouts: 21.7 us -> 3.03 us
  Pallas kernels: 0 us -> 16.4 us
  blocking collectives: 11.7 us -> 0 us
  between operations: 13.9 us -> 3.42 us
  starting transfers between devices: 3.15 us -> 12.9 us
  other arithmetic: 8.86 us -> 3.77 us
    reduce_scatter x3 -> x0, waiting for transfers between devices: 107 us -> none  [the longest x1 72.2 us: shards(): lax.psum_scatter(lax.dot_general(incoming, key_gradient, (((0,), (0,)), (...]
    ppermute x1 -> x12, waiting for transfers between devices: 0.01 us -> 41.7 us  [the longest x8 26.8 us: swapped(): return lax.ppermute(block, axis, [(i, i ^ mask) for i in range(count)])]
    dot_general x49 -> x0, matrix products: 29.8 us -> none  [the longest x8 6.78 us: advance(): jnp.einsum('rd,kd->rk', block_query, keys_one, preferred_element_type=jnp...]
    pallas_call x0 -> x2, Pallas kernels: none -> 16.4 us  [the longest x1 9.4 us: attention(): pl.pallas_call(functools.partial(attention_kernel, count, group, scaling)...]
    all_gather x2 -> x0, blocking collectives: 11.7 us -> none  [the longest x1 5.91 us: shards(): lax.all_gather(key_cube, 'ctx', axis=0, tiled=True)]
    ppermute x1 -> x12, starting transfers between devices: 3.03 us -> 12.9 us  [the longest x8 8.57 us: swapped(): return lax.ppermute(block, axis, [(i, i ^ mask) for i in range(count)])]
    unnamed x20 -> x28, local copies, waits for them, and re-layouts: 10 us -> 2.12 us
    while x18 -> x0, local copies, waits for them, and re-layouts: 3.44 us -> none
  transfers between devices with their start and end apart: 4 -> 12, of which waited for: 3 -> 6; matrix products, arithmetic and copies ran while one was open for 27% -> 5% of each run, Pallas kernels for 0% -> 0%
where the time goes in v1:
time: 82.4 us; the launch traced here: 81.2 us
  waiting for transfers between devices  41.7 us (51%)
  Pallas kernels  16.4 us (20%)
  starting transfers between devices  12.9 us (16%)
  other arithmetic  3.77 us (5%)
  between operations  3.42 us (4%)
  local copies, waits for them, and re-layouts  3.03 us (4%)
    ppermute x8, waiting for transfers between devices, swapped(): return lax.ppermute(block, axis, [(i, i ^ mask) for i in range(count)])  26.8 us
    ppermute x4, waiting for transfers between devices, handed_on(): return lax.ppermute(block, (section_axis, token_axis), route)  14.9 us
    pallas_call x1, Pallas kernels, attention(): pl.pallas_call(functools.partial(attention_kernel, count, group, scaling)...  9.4 us
    ppermute x8, starting transfers between devices, swapped(): return lax.ppermute(block, axis, [(i, i ^ mask) for i in range(count)])  8.57 us
    pallas_call x1, Pallas kernels, weight_product(): pl.pallas_call(functools.partial(weight_kernel, len(incoming)), grid=(fea...  6.97 us
    ppermute x4, starting transfers between devices, handed_on(): return lax.ppermute(block, (section_axis, token_axis), route)  4.33 us
    unnamed x28, local copies, waits for them, and re-layouts  2.12 us
  transfers between devices with their start and end apart: 12, of which 6 were waited for; matrix products, arithmetic and copies ran while one was open for 5% of the time, Pallas kernels for 0%

profile of v1, /device:TPU:0, one launch (start us, length us, event | category | flops | bytes accessed | tf_op | source)
XLA Modules:
  0.0 81.2 jit_solution(12349395377732171314)
XLA Ops:
  0.6 0.9 %pad_maximum_fusion.rest_0_ = bf16[256,256]{1,0:T(8,128)(2,1)S(1)} fusion(bf16[128,256]{1,0:T(8,128)(2,1)} %bitcast.46, bf16[128,256]{1,0:T(8,128)(2,1)} %bitcast.47), kind=kLoop, calls=%fused_computation.14 | loop fusion | flops 262144 | bytes 262144 | tf_op jit(solution)/shard_map/concatenate | solution.py:222
  1.5 3.1 %collective-permute-start.1 = (bf16[256,256]{1,0:T(8,128)(2,1)S(1)}, bf16[256,256]{1,0:T(8,128)(2,1)S(1)}, u32[]{:S(2)}, u32[]{:S(2)}) collective-permute-start(bf16[256,256]{1,0:T(8,128)(2,1)S(1)} %pad_maximum_fusion.rest_0_), channel_id=1, source_target_pairs={{0,8},{4,12},{8,0},{12,4},{1,9},{5,13},{9,1},{13,5},{2,10},{6,14},... | collective-permute-start | bytes 393224 | tf_op jit(solution)/shard_map/ppermute | solution.py:27
  4.6 0.9 %convert_reduce_fusion = s32[3]{0:T(128)S(1)} fusion(s32[512]{0:T(512)} %bitcast.48, s32[3]{0:T(128)S(1)} %iota_add_fusion), kind=kLoop, calls=%fused_computation.19 | loop fusion | flops 4605 | bytes 2072 | tf_op jit(solution)/shard_map/reduce_sum | solution.py:234
  5.5 2.6 %collective-permute-done.1.rest_2_ = bf16[256,256]{1,0:T(8,128)(2,1)S(1)} collective-permute-done((bf16[256,256]{1,0:T(8,128)(2,1)S(1)}, bf16[256,256]{1,0:T(8,128)(2,1)S(1)}, u32[]{:S(2)}, u32[]{:S(2)}) %collective-permute-start.1) | collective-permute-done | bytes 131104 | tf_op jit(solution)/shard_map/ppermute | solution.py:27
  8.1 0.6 fusion.5
  11.3 0.7 pad_add_fusion.facts
  12.0 0.6 copy-done.11
  12.7 9.4 %attention_back.1 = (bf16[128,4096]{1,0:T(8,128)(2,1)}, f32[256,256]{1,0:T(8,128)}, bf16[256,256]{1,0:T(8,128)(2,1)}, f32[256,256]{1,0:T(8,128)}, bf16[256,256]{1,0:T(8,128)(2,1)}) custom-call(s32[5]{0:T(128)} %pad_add_fusion.facts, bf16[128,4096]{1,0:T(8,128)(2,1)} %bitcast.49, bf16[128,4096]{1,0:T(8,128)(2,1)} %bitcast.50, bf16[256,256]{1,0:T(8,128)(2,1)} %copy-done.9, ...), custom_call_target="tpu_custom_call" | custom-call | flops 2684354560 | bytes 4194304 | tf_op jit(solution)/shard_map/attention_back/pallas_call | solution.py:149
  22.1 1.5 %collective-permute-start.3 = (bf16[256,256]{1,0:T(8,128)(2,1)}, bf16[256,256]{1,0:T(8,128)(2,1)S(1)}, u32[]{:S(2)}, u32[]{:S(2)}) collective-permute-start(bf16[256,256]{1,0:T(8,128)(2,1)} %get-tuple-element.11), channel_id=1, source_target_pairs={{0,4},{4,0},{8,12},{12,8},{1,5},{5,1},{9,13},{13,9},{2,6},{6,2},{1... | collective-permute-start | bytes 393224 | tf_op jit(solution)/shard_map/ppermute | solution.py:27
  23.8 2.4 %collective-permute-start.10 = (bf16[128,2048]{1,0:T(8,128)(2,1)S(1)}, bf16[128,2048]{1,0:T(8,128)(2,1)S(1)}, u32[]{:S(2)}, u32[]{:S(2)}) collective-permute-start(bf16[128,2048]{1,0:T(8,128)(2,1)S(1)} %get-tuple-element.14), channel_id=1, source_target_pairs={{0,28},{4,24},{8,20},{12,16},{16,12},{20,8},{24,4},{28,0},{1,29},{... | collective-permute-start | bytes 1572872 | tf_op jit(solution)/shard_map/ppermute | solution.py:37
  26.6 1.5 %collective-permute-start.7 = (bf16[128,2048]{1,0:T(8,128)(2,1)S(1)}, bf16[128,2048]{1,0:T(8,128)(2,1)S(1)}, u32[]{:S(2)}, u32[]{:S(2)}) collective-permute-start(bf16[128,2048]{1,0:T(8,128)(2,1)S(1)} %get-tuple-element.16), channel_id=1, source_target_pairs={{0,16},{4,20},{8,24},{12,28},{16,0},{20,4},{24,8},{28,12},{1,17},{... | collective-permute-start | bytes 1572872 | tf_op jit(solution)/shard_map/ppermute | solution.py:37
  28.2 0.6 collective-permute-start.5
  28.9 0.9 %collective-permute-done.5 = bf16[256,256]{1,0:T(8,128)(2,1)S(1)} collective-permute-done((bf16[256,256]{1,0:T(8,128)(2,1)S(1)}, bf16[256,256]{1,0:T(8,128)(2,1)S(1)}, u32[]{:S(2)}, u32[]{:S(2)}) %collective-permute-start.5) | collective-permute-done | bytes 131104 | tf_op jit(solution)/shard_map/ppermute | solution.py:27
  29.8 1.6 %collective-permute-start.6 = (bf16[128,256]{1,0:T(8,128)(2,1)S(1)}, bf16[128,256]{1,0:T(8,128)(2,1)S(1)}, u32[]{:S(2)}, u32[]{:S(2)}) collective-permute-start(bf16[128,256]{1,0:T(8,128)(2,1)S(1)} %fusion.4), channel_id=1, source_target_pairs={{0,8},{4,12},{8,0},{12,4},{1,9},{5,13},{9,1},{13,5},{2,10},{6,14},... | collective-permute-start | bytes 196616 | tf_op jit(solution)/shard_map/ppermute | solution.py:27
  31.5 20.2 %collective-permute-done.6 = bf16[128,256]{1,0:T(8,128)(2,1)S(1)} collective-permute-done((bf16[128,256]{1,0:T(8,128)(2,1)S(1)}, bf16[128,256]{1,0:T(8,128)(2,1)S(1)}, u32[]{:S(2)}, u32[]{:S(2)}) %collective-permute-start.6) | collective-permute-done | bytes 65568 | tf_op jit(solution)/shard_map/ppermute | solution.py:27
  51.7 1.7 %collective-permute-start.4 = (bf16[256,256]{1,0:T(8,128)(2,1)S(1)}, bf16[256,256]{1,0:T(8,128)(2,1)S(1)}, u32[]{:S(2)}, u32[]{:S(2)}) collective-permute-start(bf16[256,256]{1,0:T(8,128)(2,1)S(1)} %pad_maximum_fusion.1), channel_id=1, source_target_pairs={{0,8},{4,12},{8,0},{12,4},{1,9},{5,13},{9,1},{13,5},{2,10},{6,14},... | collective-permute-start | bytes 393224 | tf_op jit(solution)/shard_map/ppermute | solution.py:27
  53.4 0.6 fusion.3
  54.0 3.1 %collective-permute-done.4 = bf16[256,256]{1,0:T(8,128)(2,1)S(1)} collective-permute-done((bf16[256,256]{1,0:T(8,128)(2,1)S(1)}, bf16[256,256]{1,0:T(8,128)(2,1)S(1)}, u32[]{:S(2)}, u32[]{:S(2)}) %collective-permute-start.4) | collective-permute-done | bytes 131104 | tf_op jit(solution)/shard_map/ppermute | solution.py:27
  57.2 0.6 slice_bitcast_fusion.3
  57.9 4.1 %collective-permute-done.7.refs_0_ = bf16[128,2048]{1,0:T(8,128)(2,1)S(1)} collective-permute-done((bf16[128,2048]{1,0:T(8,128)(2,1)S(1)}, bf16[128,2048]{1,0:T(8,128)(2,1)S(1)}, u32[]{:S(2)}, u32[]{:S(2)}) %collective-permute-start.7) | collective-permute-done | bytes 524320 | tf_op jit(solution)/shard_map/ppermute | solution.py:37
  62.0 10.8 %collective-permute-done.9.refs_2_ = bf16[128,2048]{1,0:T(8,128)(2,1)S(1)} collective-permute-done((bf16[128,2048]{1,0:T(8,128)(2,1)S(1)}, bf16[128,2048]{1,0:T(8,128)(2,1)S(1)}, u32[]{:S(2)}, u32[]{:S(2)}) %collective-permute-start.9) | collective-permute-done | bytes 524320 | tf_op jit(solution)/shard_map/ppermute | solution.py:37
  72.9 0.7 copy-done.5
  73.6 0.6 copy-done.8
  74.3 7.0 %weight_product.1 = f32[2048,256]{1,0:T(8,128)} custom-call(bf16[128,2048]{1,0:T(8,128)(2,1)} %copy-done.4, bf16[128,2048]{1,0:T(8,128)(2,1)} %copy-done.3, bf16[128,2048]{1,0:T(8,128)(2,1)} %copy-done.5, bf16[128,2048]{1,0:T(8,128)(2,1)} %copy-done.2, bf16[256,256]{1,0:T(8,128)(2,1)} %copy-done.1, bf16[256,256]{1,0:T(8,128)(2,1)} %copy-done.8), custom_call_target="tpu_custom_call" | custom-call | flops 536870912 | bytes 4194304 | tf_op jit(solution)/shard_map/weight_product/pallas_call | solution.py:198
  (45 shorter events, 1.0 us)
Async XLA Ops:
  1.5 10.5 %copy-start.9 = (bf16[256,256]{1,0:T(8,128)(2,1)}, bf16[256,256]{1,0:T(8,128)(2,1)S(1)}, u32[]{:S(2)}) copy-start(bf16[256,256]{1,0:T(8,128)(2,1)S(1)} %pad_maximum_fusion.rest_0_) | copy-start | bytes 393220
  1.5 6.6 %collective-permute-start.1 = (bf16[256,256]{1,0:T(8,128)(2,1)S(1)}, bf16[256,256]{1,0:T(8,128)(2,1)S(1)}, u32[]{:S(2)}, u32[]{:S(2)}) collective-permute-start(bf16[256,256]{1,0:T(8,128)(2,1)S(1)} %pad_maximum_fusion.rest_0_), channel_id=1, source_target_pairs={{0,8},{4,12},{8,0},{12,4},{1,9},{5,13},{9,1},{13,5},{2,10},{6,14},... | collective-permute-start | bytes 393224 | tf_op jit(solution)/shard_map/ppermute | solution.py:27
  4.6 7.4 %collective-permute-start = (bf16[256,256]{1,0:T(8,128)(2,1)S(1)}, bf16[256,256]{1,0:T(8,128)(2,1)S(1)}, u32[]{:S(2)}, u32[]{:S(2)}) collective-permute-start(bf16[256,256]{1,0:T(8,128)(2,1)S(1)} %pad_maximum_fusion.rest_0_), channel_id=1, source_target_pairs={{0,4},{4,0},{8,12},{12,8},{1,5},{5,1},{9,13},{13,9},{2,6},{6,2},{1... | collective-permute-start | bytes 393224 | tf_op jit(solution)/shard_map/ppermute | solution.py:27
  8.1 3.9 %copy-start.10 = (bf16[256,256]{1,0:T(8,128)(2,1)}, bf16[256,256]{1,0:T(8,128)(2,1)S(1)}, u32[]{:S(2)}) copy-start(bf16[256,256]{1,0:T(8,128)(2,1)S(1)} %collective-permute-done.1.rest_2_) | copy-start | bytes 393220
  8.1 3.9 %collective-permute-start.2 = (bf16[256,256]{1,0:T(8,128)(2,1)S(1)}, bf16[256,256]{1,0:T(8,128)(2,1)S(1)}, u32[]{:S(2)}, u32[]{:S(2)}) collective-permute-start(bf16[256,256]{1,0:T(8,128)(2,1)S(1)} %collective-permute-done.1.rest_2_), channel_id=1, source_target_pairs={{0,4},{4,0},{8,12},{12,8},{1,5},{5,1},{9,13},{13,9},{2,6},{6,2},{1... | collective-permute-start | bytes 393224 | tf_op jit(solution)/shard_map/ppermute | solution.py:27
  12.0 0.7 copy-start.12
  12.7 10.9 %copy-start = (bf16[1,128,8192]{2,1,0:T(8,128)(2,1)S(1)}, bf16[1,128,8192]{2,1,0:T(8,128)(2,1)}, u32[]{:S(2)}) copy-start(bf16[1,128,8192]{2,1,0:T(8,128)(2,1)} %param.10) | copy-start | bytes 6291460
  22.1 6.1 %copy-start.13 = (bf16[256,256]{1,0:T(8,128)(2,1)S(1)}, bf16[256,256]{1,0:T(8,128)(2,1)}, u32[]{:S(2)}) copy-start(bf16[256,256]{1,0:T(8,128)(2,1)} %get-tuple-element.13) | copy-start | bytes 393220
  22.1 6.7 %copy-start.7 = (f32[256,256]{1,0:T(8,128)S(1)}, f32[256,256]{1,0:T(8,128)}, u32[]{:S(2)}) copy-start(f32[256,256]{1,0:T(8,128)} %get-tuple-element.10) | copy-start | bytes 786436
  22.1 7.7 %copy-start.6 = (f32[256,256]{1,0:T(8,128)S(1)}, f32[256,256]{1,0:T(8,128)}, u32[]{:S(2)}) copy-start(f32[256,256]{1,0:T(8,128)} %get-tuple-element.12) | copy-start | bytes 786436
  22.1 6.0 %collective-permute-start.3 = (bf16[256,256]{1,0:T(8,128)(2,1)}, bf16[256,256]{1,0:T(8,128)(2,1)S(1)}, u32[]{:S(2)}, u32[]{:S(2)}) collective-permute-start(bf16[256,256]{1,0:T(8,128)(2,1)} %get-tuple-element.11), channel_id=1, source_target_pairs={{0,4},{4,0},{8,12},{12,8},{1,5},{5,1},{9,13},{13,9},{2,6},{6,2},{1... | collective-permute-start | bytes 393224 | tf_op jit(solution)/shard_map/ppermute | solution.py:27
  23.8 34.0 %collective-permute-start.10 = (bf16[128,2048]{1,0:T(8,128)(2,1)S(1)}, bf16[128,2048]{1,0:T(8,128)(2,1)S(1)}, u32[]{:S(2)}, u32[]{:S(2)}) collective-permute-start(bf16[128,2048]{1,0:T(8,128)(2,1)S(1)} %get-tuple-element.14), channel_id=1, source_target_pairs={{0,28},{4,24},{8,20},{12,16},{16,12},{20,8},{24,4},{28,0},{1,29},{... | collective-permute-start | bytes 1572872 | tf_op jit(solution)/shard_map/ppermute | solution.py:37
  26.2 31.7 %collective-permute-start.8 = (bf16[128,2048]{1,0:T(8,128)(2,1)S(1)}, bf16[128,2048]{1,0:T(8,128)(2,1)S(1)}, u32[]{:S(2)}, u32[]{:S(2)}) collective-permute-start(bf16[128,2048]{1,0:T(8,128)(2,1)S(1)} %get-tuple-element.15), channel_id=1, source_target_pairs={{0,24},{4,28},{8,16},{12,20},{16,8},{20,12},{24,0},{28,4},{1,25},{... | collective-permute-start | bytes 1572872 | tf_op jit(solution)/shard_map/ppermute | solution.py:37
  26.6 35.4 %collective-permute-start.7 = (bf16[128,2048]{1,0:T(8,128)(2,1)S(1)}, bf16[128,2048]{1,0:T(8,128)(2,1)S(1)}, u32[]{:S(2)}, u32[]{:S(2)}) collective-permute-start(bf16[128,2048]{1,0:T(8,128)(2,1)S(1)} %get-tuple-element.16), channel_id=1, source_target_pairs={{0,16},{4,20},{8,24},{12,28},{16,0},{20,4},{24,8},{28,12},{1,17},{... | collective-permute-start | bytes 1572872 | tf_op jit(solution)/shard_map/ppermute | solution.py:37
  28.2 44.7 %collective-permute-start.9 = (bf16[128,2048]{1,0:T(8,128)(2,1)S(1)}, bf16[128,2048]{1,0:T(8,128)(2,1)S(1)}, u32[]{:S(2)}, u32[]{:S(2)}) collective-permute-start(bf16[128,2048]{1,0:T(8,128)(2,1)S(1)} %get-tuple-element.17), channel_id=1, source_target_pairs={{0,20},{4,16},{8,28},{12,24},{16,4},{20,0},{24,12},{28,8},{1,21},{... | collective-permute-start | bytes 1572872 | tf_op jit(solution)/shard_map/ppermute | solution.py:37
  28.2 1.6 %collective-permute-start.5 = (bf16[256,256]{1,0:T(8,128)(2,1)S(1)}, bf16[256,256]{1,0:T(8,128)(2,1)S(1)}, u32[]{:S(2)}, u32[]{:S(2)}) collective-permute-start(bf16[256,256]{1,0:T(8,128)(2,1)S(1)} %copy-done.13), channel_id=1, source_target_pairs={{0,4},{4,0},{8,12},{12,8},{1,5},{5,1},{9,13},{13,9},{2,6},{6,2},{1... | collective-permute-start | bytes 393224 | tf_op jit(solution)/shard_map/ppermute | solution.py:27
  29.8 21.8 %collective-permute-start.6 = (bf16[128,256]{1,0:T(8,128)(2,1)S(1)}, bf16[128,256]{1,0:T(8,128)(2,1)S(1)}, u32[]{:S(2)}, u32[]{:S(2)}) collective-permute-start(bf16[128,256]{1,0:T(8,128)(2,1)S(1)} %fusion.4), channel_id=1, source_target_pairs={{0,8},{4,12},{8,0},{12,4},{1,9},{5,13},{9,1},{13,5},{2,10},{6,14},... | collective-permute-start | bytes 196616 | tf_op jit(solution)/shard_map/ppermute | solution.py:27
  51.7 5.5 %collective-permute-start.4 = (bf16[256,256]{1,0:T(8,128)(2,1)S(1)}, bf16[256,256]{1,0:T(8,128)(2,1)S(1)}, u32[]{:S(2)}, u32[]{:S(2)}) collective-permute-start(bf16[256,256]{1,0:T(8,128)(2,1)S(1)} %pad_maximum_fusion.1), channel_id=1, source_target_pairs={{0,8},{4,12},{8,0},{12,4},{1,9},{5,13},{9,1},{13,5},{2,10},{6,14},... | collective-permute-start | bytes 393224 | tf_op jit(solution)/shard_map/ppermute | solution.py:27
  57.2 15.7 %copy-start.1 = (bf16[256,256]{1,0:T(8,128)(2,1)}, bf16[256,256]{1,0:T(8,128)(2,1)S(1)}, u32[]{:S(2)}) copy-start(bf16[256,256]{1,0:T(8,128)(2,1)S(1)} %fusion.refs_4_) | copy-start | bytes 393220
  57.2 15.7 %collective-permute-start.11 = (bf16[256,256]{1,0:T(8,128)(2,1)S(1)}, bf16[256,256]{1,0:T(8,128)(2,1)S(1)}, u32[]{:S(2)}, u32[]{:S(2)}) collective-permute-start(bf16[256,256]{1,0:T(8,128)(2,1)S(1)} %fusion.refs_4_), channel_id=1, source_target_pairs={{0,4},{4,0},{8,12},{12,8},{1,5},{5,1},{9,13},{13,9},{2,6},{6,2},{1... | collective-permute-start | bytes 393224 | tf_op jit(solution)/shard_map/ppermute | solution.py:27
  57.9 15.0 %copy-start.2 = (bf16[128,2048]{1,0:T(8,128)(2,1)}, bf16[128,2048]{1,0:T(8,128)(2,1)S(1)}, u32[]{:S(2)}) copy-start(bf16[128,2048]{1,0:T(8,128)(2,1)S(1)} %collective-permute-done.10.refs_3_) | copy-start | bytes 1572868
  57.9 15.0 %copy-start.3 = (bf16[128,2048]{1,0:T(8,128)(2,1)}, bf16[128,2048]{1,0:T(8,128)(2,1)S(1)}, u32[]{:S(2)}) copy-start(bf16[128,2048]{1,0:T(8,128)(2,1)S(1)} %collective-permute-done.8.refs_1_) | copy-start | bytes 1572868
  62.0 10.8 %copy-start.4 = (bf16[128,2048]{1,0:T(8,128)(2,1)}, bf16[128,2048]{1,0:T(8,128)(2,1)S(1)}, u32[]{:S(2)}) copy-start(bf16[128,2048]{1,0:T(8,128)(2,1)S(1)} %collective-permute-done.7.refs_0_) | copy-start | bytes 1572868
  72.8 0.8 copy-start.5
  (2 other events, 1.3 us)
